TPU v7x, 256 devices: a whole 4x4x8 slice. The times are simulated.
256 devices in a mesh: cuts: 16 (over z, core), rank: 16 (over x, y).
Axes of the slice: x: 4, y: 4, z: 8, core: 2. Of those that a mesh axis runs over, the one named last changes fastest.
Arguments:
- core_one: float32 [512, 320, 512], P('rank', 'cuts'), may hold values from -6 to 6
- core_two: float32 [512, 320, 512], P('rank', 'cuts'), may hold values from -0.25 to 0.25
- right_sketch: float32 [512, 128], replicated, may hold values from -0.25 to 0.25
- sketch_core: float32 [128, 320, 128], P(None, 'cuts'), may hold values from -0.03125 to 0.03125
Outputs:
- left_core: float32 [512, 320, 128], P('rank', 'cuts')
- middle_core: float32 [128, 320, 128], P('rank', 'cuts')
- carry: float32 [128, 512], replicated
All inputs are finite; a program needn't handle non-finite values.
Results may differ from a plain program's by a relative error of at most 0.00015.
Values sent between devices are 32-bit elements; how exact they have to be, the bound alone decides.
A program may use at most 64 MiB of HBM per device.

v0:
```python
import jax
import jax.numpy as jnp
from jax import lax
from jax.sharding import PartitionSpec as P

R = 512
NM = 320
L = 128


def orthonormalize(all_rows, own_rows, carry_of):
    highest = lax.Precision.HIGHEST
    local_gram = jnp.dot(
        own_rows.T, own_rows, precision=highest, preferred_element_type=jnp.float32
    )
    gram = lax.psum(local_gram, ("cuts", "rank"))
    factor = jnp.linalg.cholesky(gram)
    ortho = lax.linalg.triangular_solve(
        factor, all_rows, left_side=False, lower=True, transpose_a=True
    )
    carried = lax.psum(carry_of(ortho), ("cuts", "rank"))
    return (ortho, carried)


def on_device(core_one, core_two, right_sketch, sketch_core):
    highest = lax.Precision.HIGHEST
    local_rows, slices, width = core_one.shape
    sketch_width = right_sketch.shape[1]
    band = sketch_width // lax.axis_size("rank")
    sketched = jnp.einsum("anj,jc->anc", core_two, right_sketch, precision=highest)
    part_bridge = jnp.einsum("anc,bnc->ab", sketched, sketch_core, precision=highest)
    bridge_rows = lax.psum(part_bridge, "cuts")
    flat_one = core_one.reshape(local_rows * slices, width)
    first_rows = jnp.dot(
        flat_one,
        lax.all_gather(bridge_rows, "rank", axis=0, tiled=True),
        precision=highest,
        preferred_element_type=jnp.float32,
    )

    def first_carry_of(matrix):
        return jnp.dot(matrix.T, flat_one, precision=highest, preferred_element_type=jnp.float32)

    first_q, first_carry = orthonormalize(first_rows, first_rows, first_carry_of)
    left_core = (jnp.sqrt(jnp.float32(R * NM)) * first_q).reshape(local_rows, slices, sketch_width)
    offset = lax.axis_index("rank") * local_rows
    local_carry = lax.dynamic_slice_in_dim(first_carry, offset, local_rows, 1)
    projected = lax.psum_scatter(
        jnp.einsum("ba,ank->bnk", local_carry, core_two, precision=highest),
        "rank",
        scatter_dimension=0,
        tiled=True,
    )
    flat_two = projected.reshape(band * slices, width)
    second_rows = jnp.dot(
        flat_two, right_sketch, precision=highest, preferred_element_type=jnp.float32
    )

    def second_carry_of(matrix):
        return jnp.dot(matrix.T, flat_two, precision=highest, preferred_element_type=jnp.float32)

    second_flat, carry = orthonormalize(second_rows, second_rows, second_carry_of)
    second_q = second_flat.reshape(band, slices, sketch_width)
    middle_core = jnp.sqrt(jnp.float32(L * NM)) * second_q
    return (left_core, middle_core, carry)


def solution(mesh):
    placed = (P("rank", "cuts", None), P("rank", "cuts", None), P(), P(None, "cuts", None))
    return jax.shard_map(
        on_device,
        mesh=mesh,
        in_specs=placed,
        out_specs=(P("rank", "cuts", None), P("rank", "cuts", None), P()),
        check_vma=False,
    )
```

profile of v0, /device:TPU:2, one launch (start us, length us, event | category | flops | bytes accessed | tf_op | source)
XLA Modules:
  0.0 1233.6 jit_solution(7768651899658973247)
XLA Ops:
  7.2 0.0 copy-start
  7.2 0.0 copy-start.1
  7.2 0.0 all-reduce.5.cloned.1.call-start
  7.2 1.3 copy-done
  8.5 2.1 fusion
  10.6 0.0 copy-done.1
  10.6 1.4 convolution_bitcast_fusion
  12.0 50.9 %psum.35 = f32[32,128]{1,0:T(8,128)S(1)} all-reduce(f32[32,128]{1,0:T(8,128)S(1)} %convolution_bitcast_fusion), channel_id=1, replica_groups=mesh['cuts'=16,'rank'=16] {'cuts'}, use_global_device_ids=true, to_apply=%region_0.0 | all-reduce | flops 4096 | bytes 32768 | tf_op jit(solution)/shard_map/psum | solution.py:32
  62.9 23.8 %all_gather.3 = f32[512,128]{1,0:T(8,128)S(1)} all-gather(f32[32,128]{1,0:T(8,128)S(1)} %psum.35), channel_id=1, replica_groups=mesh['cuts'=16,'rank'=16] {'rank'}, dimensions={0}, use_global_device_ids=true | all-gather | bytes 278528 | tf_op jit(solution)/shard_map/all_gather | solution.py:36
  86.7 3.2 copy.13
  89.9 1.5 reshape.29
  91.4 1.6 fusion.14
  92.9 1.1 fusion.15
  94.0 0.0 all-reduce.5.cloned.1.call-update
  94.1 0.2 all-reduce.7.cloned.1.call-start
  94.3 236.5 %all-reduce.5.cloned.1.call-done = f32[128,128]{0,1:T(8,128)} async-done(((f32[128,128]{0,1:T(8,128)}), f32[128,128]{0,1:T(8,128)}) %all-reduce.5.cloned.1.call-update) | async-done | bytes 65552 | tf_op jit(solution)/shard_map/psum | solution.py:16
  330.8 0.9 copy.15
  331.8 0.9 fusion.9
  332.6 11.7 cholesky.44
  344.4 0.6 compare_reduce_fusion.1
  345.0 0.7 fusion.2
  345.7 9.8 custom-call.8
  355.5 0.7 broadcast_multiply_fusion
  356.2 3.0 fusion.16
  359.2 0.0 all-reduce.7.cloned.1.call-update
  359.2 0.0 reduce-scatter.2.cloned.1.call-start
  359.2 251.8 %all-reduce.7.cloned.1.call-done = f32[128,512]{0,1:T(8,128)} async-done(((f32[128,512]{0,1:T(8,128)}), f32[128,512]{0,1:T(8,128)}) %all-reduce.7.cloned.1.call-update) | async-done | bytes 262160 | tf_op jit(solution)/shard_map/psum | solution.py:21
  611.0 6.8 fusion.10
  617.8 0.0 reduce-scatter.2.cloned.1.call-update
  617.8 0.0 copy-start.2
  617.8 0.3 all-reduce.9.cloned.1.call-start
  618.1 83.2 %reduce-scatter.2.cloned.1.call-done = f32[8,20,512]{2,0,1:T(8,128)} async-done(((f32[128,20,512]{2,0,1:T(8,128)}), f32[8,20,512]{2,0,1:T(8,128)}) %reduce-scatter.2.cloned.1.call-update) | async-done | bytes 327696 | tf_op jit(solution)/shard_map/reduce_scatter | solution.py:48
  701.3 1.2 copy.16
  702.5 0.0 copy-done.2
  702.5 0.4 fusion.17
  703.0 1.1 fusion.18
  704.0 0.0 all-reduce.9.cloned.1.call-update
  704.1 0.0 all-reduce.11.cloned.1.call-start
  704.1 243.4 %all-reduce.9.cloned.1.call-done = f32[128,128]{0,1:T(8,128)} async-done(((f32[128,128]{0,1:T(8,128)}), f32[128,128]{0,1:T(8,128)}) %all-reduce.9.cloned.1.call-update) | async-done | bytes 65552 | tf_op jit(solution)/shard_map/psum | solution.py:16
  947.6 0.9 copy.18
  948.5 0.9 fusion.6
  949.3 11.7 cholesky.55
  961.1 0.6 compare_reduce_fusion
  961.7 0.7 fusion.3
  962.4 9.8 custom-call.9
  972.2 0.2 broadcast_multiply_fusion.1
  972.4 1.1 fusion.19
  973.6 0.0 all-reduce.11.cloned.1.call-update
  973.6 0.8 copy.19
  974.4 0.7 copy.20
  975.1 250.3 %all-reduce.11.cloned.1.call-done = f32[128,512]{1,0:T(8,128)} async-done(((f32[128,512]{1,0:T(8,128)}), f32[128,512]{1,0:T(8,128)}) %all-reduce.11.cloned.1.call-update) | async-done | bytes 262160 | tf_op jit(solution)/shard_map/psum | solution.py:21
  1225.4 1.7 copy.29
  (5 shorter events, 0.1 us)
Async XLA Ops:
  7.2 1.3 copy-start
  7.2 3.4 copy-start.1
  7.2 323.6 %all-reduce.5.cloned.1.call-start = ((), (), s32[]{:S(2)}) async-start(), calls=%async_computation.1 | async-start | bytes 131072 | tf_op jit(solution)/shard_map/psum | solution.py:16
  94.1 516.9 %all-reduce.7.cloned.1.call-start = ((), (), s32[]{:S(2)}) async-start(), calls=%async_computation.2 | async-start | bytes 524288 | tf_op jit(solution)/shard_map/psum | solution.py:21
  359.2 342.1 %reduce-scatter.2.cloned.1.call-start = ((), (), s32[]{:S(2)}) async-start(), calls=%async_computation.3 | async-start | bytes 5570560 | tf_op jit(solution)/shard_map/reduce_scatter | solution.py:48
  617.8 84.7 %copy-start.2 = (f32[512,128]{1,0:T(8,128)S(1)}, f32[512,128]{1,0:T(8,128)}, u32[]{:S(2)}) copy-start(f32[512,128]{1,0:T(8,128)} %param.7) | copy-start | bytes 786436
  617.8 329.7 %all-reduce.9.cloned.1.call-start = ((), (), s32[]{:S(2)}) async-start(), calls=%async_computation.4 | async-start | bytes 131072 | tf_op jit(solution)/shard_map/psum | solution.py:16
  704.1 521.3 %all-reduce.11.cloned.1.call-start = ((), (), s32[]{:S(2)}) async-start(), calls=%async_computation.5 | async-start | bytes 524288 | tf_op jit(solution)/shard_map/psum | solution.py:21
Sparse Core Ops, SparseCore 0:
  94.2 236.5 all-reduce.4
  359.3 251.6 all-reduce.6
  617.9 83.3 reduce-scatter.1
  707.3 240.2 all-reduce.8
  973.7 251.5 all-reduce.10
where the time goes:
time: 1230 us
  waiting for transfers between devices  1070 us (87%)
  blocking collectives  74.6 us (6%)
  other arithmetic  47.4 us (4%)
  matrix products  19.5 us (2%)
  between operations  13.9 us (1%)
    psum x2, waiting for transfers between devices, orthonormalize(): carried = lax.psum(carry_of(ortho), ('cuts', 'rank'))  502 us
    psum x2, waiting for transfers between devices, orthonormalize(): gram = lax.psum(local_gram, ('cuts', 'rank'))  480 us
    reduce_scatter x1, waiting for transfers between devices, on_device(): lax.psum_scatter(jnp.einsum('ba,ank->bnk', local_carry, core_two, precisi...  83.2 us
    psum x1, blocking collectives, on_device(): bridge_rows = lax.psum(part_bridge, 'cuts')  50.9 us
    another operation x6, other arithmetic, orthonormalize(): factor = jnp.linalg.cholesky(gram)  24.8 us
  transfers between devices with their start and end apart: 5, of which 5 were waited for; matrix products, arithmetic and copies ran while one was open for 0% of the time, Pallas kernels for 0%

commit v1 on v0

--- a/solution.py
+++ b/solution.py
@@ -8,12 +8,17 @@
 L = 128
 
 
+def by_each_axis(array, axis_one, axis_two):
+    inner = lax.psum(array, axis_one)
+    return lax.psum(inner, axis_two)
+
+
 def orthonormalize(all_rows, own_rows, carry_of):
     highest = lax.Precision.HIGHEST
     local_gram = jnp.dot(
         own_rows.T, own_rows, precision=highest, preferred_element_type=jnp.float32
     )
-    gram = lax.psum(local_gram, ("cuts", "rank"))
+    gram = by_each_axis(local_gram, "rank", "cuts")
     factor = jnp.linalg.cholesky(gram)
     ortho = lax.linalg.triangular_solve(
         factor, all_rows, left_side=False, lower=True, transpose_a=True

time: 1230 us -> 1140 us (0.927)
  waiting for transfers between devices: 1070 us -> 973 us
    psum x2 -> x4, waiting for transfers between devices: 480 us -> 385 us  [the longest x2 205 us: by_each_axis(): return lax.psum(inner, axis_two)]
  transfers between devices with their start and end apart: 5 -> 7, of which waited for: 5 -> 7; matrix products, arithmetic and copies ran while one was open for 0% -> 0% of each run, Pallas kernels for 0% -> 0%
where the time goes in v1:
time: 1140 us
  waiting for transfers between devices  973 us (85%)
  blocking collectives  74.6 us (7%)
  other arithmetic  47.4 us (4%)
  matrix products  19.5 us (2%)
  between operations  14.3 us (1%)
  local copies, waits for them, and re-layouts  12.2 us (1%)
    psum x2, waiting for transfers between devices, orthonormalize(): carried = lax.psum(carry_of(ortho), ('cuts', 'rank'))  505 us
    psum x2, waiting for transfers between devices, by_each_axis(): return lax.psum(inner, axis_two)  205 us
    psum x2, waiting for transfers between devices, by_each_axis(): inner = lax.psum(array, axis_one)  180 us
    reduce_scatter x1, waiting for transfers between devices, on_device(): lax.psum_scatter(jnp.einsum('ba,ank->bnk', local_carry, core_two, precisi...  83.2 us
    psum x1, blocking collectives, on_device(): bridge_rows = lax.psum(part_bridge, 'cuts')  50.9 us
    another operation x6, other arithmetic, orthonormalize(): factor = jnp.linalg.cholesky(gram)  24.8 us
    all_gather x1, blocking collectives, on_device(): lax.all_gather(bridge_rows, 'rank', axis=0, tiled=True)  23.8 us
  transfers between devices with their start and end apart: 7, of which 7 were waited for; matrix products, arithmetic and copies ran while one was open for 0% of the time, Pallas kernels for 0%

profile of v1, /device:TPU:2, one launch (start us, length us, event | category | flops | bytes accessed | tf_op | source)
XLA Modules:
  0.0 1142.1 jit_solution(1248734827368792865)
XLA Ops:
  7.2 0.0 copy-start
  7.2 0.0 copy-start.1
  7.2 0.0 all-reduce.7.cloned.1.call-start
  7.2 1.3 copy-done
  8.5 2.1 fusion
  10.6 0.0 copy-done.1
  10.6 1.4 convolution_bitcast_fusion
  12.0 50.9 %psum.49 = f32[32,128]{1,0:T(8,128)S(1)} all-reduce(f32[32,128]{1,0:T(8,128)S(1)} %convolution_bitcast_fusion), channel_id=1, replica_groups=mesh['cuts'=16,'rank'=16] {'cuts'}, use_global_device_ids=true, to_apply=%region_0.0 | all-reduce | flops 4096 | bytes 32768 | tf_op jit(solution)/shard_map/psum | solution.py:37
  62.9 23.8 %all_gather.3 = f32[512,128]{1,0:T(8,128)S(1)} all-gather(f32[32,128]{1,0:T(8,128)S(1)} %psum.49), channel_id=1, replica_groups=mesh['cuts'=16,'rank'=16] {'rank'}, dimensions={0}, use_global_device_ids=true | all-gather | bytes 278528 | tf_op jit(solution)/shard_map/all_gather | solution.py:41
  86.7 3.2 copy.13
  89.9 1.5 reshape.29
  91.4 1.6 fusion.14
  92.9 1.1 fusion.15
  94.0 0.0 all-reduce.7.cloned.1.call-update
  94.1 0.0 all-reduce.9.cloned.1.call-start
  94.1 87.9 %all-reduce.7.cloned.1.call-done = f32[128,128]{0,1:T(8,128)} async-done(((f32[128,128]{0,1:T(8,128)}), f32[128,128]{0,1:T(8,128)}) %all-reduce.7.cloned.1.call-update) | async-done | bytes 65552 | tf_op jit(solution)/shard_map/psum | solution.py:12
  182.0 0.0 all-reduce.9.cloned.1.call-update
  182.0 0.2 all-reduce.11.cloned.1.call-start
  182.2 102.4 %all-reduce.9.cloned.1.call-done = f32[128,128]{0,1:T(8,128)} async-done(((f32[128,128]{0,1:T(8,128)}), f32[128,128]{0,1:T(8,128)}) %all-reduce.9.cloned.1.call-update) | async-done | bytes 65552 | tf_op jit(solution)/shard_map/psum | solution.py:13
  284.7 0.9 copy.15
  285.6 0.9 fusion.9
  286.5 11.7 %cholesky.44 = f32[128,128]{1,0:T(8,128)S(1)} custom-call(f32[128,128]{1,0:T(8,128)S(1)} %fusion.9), custom_call_target="Cholesky" | custom-call | tf_op jit(solution)/shard_map/jit(cholesky)/cholesky | solution.py:22
  298.2 0.6 compare_reduce_fusion.1
  298.8 0.7 fusion.2
  299.5 9.8 custom-call.8
  309.3 0.7 broadcast_multiply_fusion
  310.0 3.0 fusion.16
  313.0 0.0 all-reduce.11.cloned.1.call-update
  313.0 0.0 reduce-scatter.2.cloned.1.call-start
  313.1 253.2 %all-reduce.11.cloned.1.call-done = f32[128,512]{0,1:T(8,128)} async-done(((f32[128,512]{0,1:T(8,128)}), f32[128,512]{0,1:T(8,128)}) %all-reduce.11.cloned.1.call-update) | async-done | bytes 262160 | tf_op jit(solution)/shard_map/psum | solution.py:26
  566.3 6.8 fusion.10
  573.1 0.0 reduce-scatter.2.cloned.1.call-update
  573.1 0.0 copy-start.2
  573.1 0.3 all-reduce.13.cloned.1.call-start
  573.4 83.2 %reduce-scatter.2.cloned.1.call-done = f32[8,20,512]{2,0,1:T(8,128)} async-done(((f32[128,20,512]{2,0,1:T(8,128)}), f32[8,20,512]{2,0,1:T(8,128)}) %reduce-scatter.2.cloned.1.call-update) | async-done | bytes 327696 | tf_op jit(solution)/shard_map/reduce_scatter | solution.py:53
  656.6 1.2 copy.16
  657.8 0.0 copy-done.2
  657.8 0.4 fusion.17
  658.2 1.1 fusion.18
  659.3 0.0 all-reduce.13.cloned.1.call-update
  659.3 0.0 all-reduce.15.cloned.1.call-start
  659.4 92.4 %all-reduce.13.cloned.1.call-done = f32[128,128]{0,1:T(8,128)} async-done(((f32[128,128]{0,1:T(8,128)}), f32[128,128]{0,1:T(8,128)}) %all-reduce.13.cloned.1.call-update) | async-done | bytes 65552 | tf_op jit(solution)/shard_map/psum | solution.py:12
  751.7 0.0 all-reduce.15.cloned.1.call-update
  751.8 0.0 all-reduce.17.cloned.1.call-start
  751.8 102.5 %all-reduce.15.cloned.1.call-done = f32[128,128]{0,1:T(8,128)} async-done(((f32[128,128]{0,1:T(8,128)}), f32[128,128]{0,1:T(8,128)}) %all-reduce.15.cloned.1.call-update) | async-done | bytes 65552 | tf_op jit(solution)/shard_map/psum | solution.py:13
  854.3 0.9 copy.18
  855.2 0.9 fusion.6
  856.1 11.7 %cholesky.55 = f32[128,128]{1,0:T(8,128)S(1)} custom-call(f32[128,128]{1,0:T(8,128)S(1)} %fusion.6), custom_call_target="Cholesky" | custom-call | tf_op jit(solution)/shard_map/jit(cholesky)/cholesky | solution.py:22
  867.8 0.6 compare_reduce_fusion
  868.5 0.7 fusion.3
  869.1 9.8 custom-call.9
  878.9 0.2 broadcast_multiply_fusion.1
  879.2 1.1 fusion.19
  880.3 0.0 all-reduce.17.cloned.1.call-update
  880.4 0.8 copy.19
  881.2 0.7 copy.20
  881.8 251.8 %all-reduce.17.cloned.1.call-done = f32[128,512]{1,0:T(8,128)} async-done(((f32[128,512]{1,0:T(8,128)}), f32[128,512]{1,0:T(8,128)}) %all-reduce.17.cloned.1.call-update) | async-done | bytes 262160 | tf_op jit(solution)/shard_map/psum | solution.py:26
  1133.6 1.7 copy.31
  (5 shorter events, 0.1 us)
Async XLA Ops:
  7.2 1.3 copy-start
  7.2 3.4 copy-start.1
  7.2 174.8 %all-reduce.7.cloned.1.call-start = ((), (), s32[]{:S(2)}) async-start(), calls=%async_computation.1 | async-start | bytes 131072 | tf_op jit(solution)/shard_map/psum | solution.py:12
  94.1 190.6 %all-reduce.9.cloned.1.call-start = ((), (), s32[]{:S(2)}) async-start(), calls=%async_computation.2 | async-start | bytes 131072 | tf_op jit(solution)/shard_map/psum | solution.py:13
  182.0 384.3 %all-reduce.11.cloned.1.call-start = ((), (), s32[]{:S(2)}) async-start(), calls=%async_computation.3 | async-start | bytes 524288 | tf_op jit(solution)/shard_map/psum | solution.py:26
  313.0 343.6 %reduce-scatter.2.cloned.1.call-start = ((), (), s32[]{:S(2)}) async-start(), calls=%async_computation.4 | async-start | bytes 5570560 | tf_op jit(solution)/shard_map/reduce_scatter | solution.py:53
  573.1 84.7 %copy-start.2 = (f32[512,128]{1,0:T(8,128)S(1)}, f32[512,128]{1,0:T(8,128)}, u32[]{:S(2)}) copy-start(f32[512,128]{1,0:T(8,128)} %param.7) | copy-start | bytes 786436
  573.1 178.6 %all-reduce.13.cloned.1.call-start = ((), (), s32[]{:S(2)}) async-start(), calls=%async_computation.5 | async-start | bytes 131072 | tf_op jit(solution)/shard_map/psum | solution.py:12
  659.3 194.9 %all-reduce.15.cloned.1.call-start = ((), (), s32[]{:S(2)}) async-start(), calls=%async_computation.6 | async-start | bytes 131072 | tf_op jit(solution)/shard_map/psum | solution.py:13
  751.8 381.9 %all-reduce.17.cloned.1.call-start = ((), (), s32[]{:S(2)}) async-start(), calls=%async_computation.7 | async-start | bytes 524288 | tf_op jit(solution)/shard_map/psum | solution.py:26
Sparse Core Ops, SparseCore 0:
  94.2 87.7 all-reduce.6
  184.3 100.3 all-reduce.8
  313.1 253.0 all-reduce.10
  573.2 83.3 reduce-scatter.1
  660.2 91.4 all-reduce.12
  753.9 100.3 all-reduce.14
  880.5 253.1 all-reduce.16

commit v2 on v0

--- a/solution.py
+++ b/solution.py
@@ -18,7 +18,11 @@
     ortho = lax.linalg.triangular_solve(
         factor, all_rows, left_side=False, lower=True, transpose_a=True
     )
-    carried = lax.psum(carry_of(ortho), ("cuts", "rank"))
+
+    def _refer_fields(vector):
+        return lax.psum(lax.psum(vector, axis_name="cuts"), axis_name="rank")
+
+    carried = _refer_fields(carry_of(ortho))
     return (ortho, carried)
 
 

time: 1230 us -> 1140 us (0.927)
  waiting for transfers between devices: 1070 us -> 974 us
    psum x2 -> x4, waiting for transfers between devices: 502 us -> 410 us  [_refer_fields(): return lax.psum(lax.psum(vector, axis_name='cuts'), axis_name='rank')]
  transfers between devices with their start and end apart: 5 -> 7, of which waited for: 5 -> 7; matrix products, arithmetic and copies ran while one was open for 0% -> 0% of each run, Pallas kernels for 0% -> 0%
where the time goes in v2:
time: 1140 us
  waiting for transfers between devices  974 us (85%)
  blocking collectives  74.6 us (7%)
  other arithmetic  47.4 us (4%)
  matrix products  19.5 us (2%)
  between operations  14.3 us (1%)
  local copies, waits for them, and re-layouts  12.2 us (1%)
    psum x2, waiting for transfers between devices, orthonormalize(): gram = lax.psum(local_gram, ('cuts', 'rank'))  480 us
    psum x4, waiting for transfers between devices, _refer_fields(): return lax.psum(lax.psum(vector, axis_name='cuts'), axis_name='rank')  410 us
    reduce_scatter x1, waiting for transfers between devices, on_device(): lax.psum_scatter(jnp.einsum('ba,ank->bnk', local_carry, core_two, precisi...  84.1 us
    psum x1, blocking collectives, on_device(): bridge_rows = lax.psum(part_bridge, 'cuts')  50.9 us
    another operation x6, other arithmetic, orthonormalize(): factor = jnp.linalg.cholesky(gram)  24.8 us
    all_gather x1, blocking collectives, on_device(): lax.all_gather(bridge_rows, 'rank', axis=0, tiled=True)  23.8 us
  transfers between devices with their start and end apart: 7, of which 7 were waited for; matrix products, arithmetic and copies ran while one was open for 0% of the time, Pallas kernels for 0%

profile of v2, /device:TPU:2, one launch (start us, length us, event | category | flops | bytes accessed | tf_op | source)
XLA Modules:
  0.0 1142.9 jit_solution(15052489077970495167)
XLA Ops:
  7.2 0.0 copy-start
  7.2 0.0 copy-start.1
  7.2 0.0 all-reduce.7.cloned.1.call-start
  7.2 1.3 copy-done
  8.5 2.1 fusion
  10.6 0.0 copy-done.1
  10.6 1.4 convolution_bitcast_fusion
  12.0 50.9 %psum.49 = f32[32,128]{1,0:T(8,128)S(1)} all-reduce(f32[32,128]{1,0:T(8,128)S(1)} %convolution_bitcast_fusion), channel_id=1, replica_groups=mesh['cuts'=16,'rank'=16] {'cuts'}, use_global_device_ids=true, to_apply=%region_0.0 | all-reduce | flops 4096 | bytes 32768 | tf_op jit(solution)/shard_map/psum | solution.py:36
  62.9 23.8 %all_gather.3 = f32[512,128]{1,0:T(8,128)S(1)} all-gather(f32[32,128]{1,0:T(8,128)S(1)} %psum.49), channel_id=1, replica_groups=mesh['cuts'=16,'rank'=16] {'rank'}, dimensions={0}, use_global_device_ids=true | all-gather | bytes 278528 | tf_op jit(solution)/shard_map/all_gather | solution.py:40
  86.7 3.2 copy.13
  89.9 1.5 reshape.29
  91.4 1.6 fusion.14
  92.9 1.1 fusion.15
  94.0 0.0 all-reduce.7.cloned.1.call-update
  94.1 0.2 all-reduce.9.cloned.1.call-start
  94.3 236.5 %all-reduce.7.cloned.1.call-done = f32[128,128]{0,1:T(8,128)} async-done(((f32[128,128]{0,1:T(8,128)}), f32[128,128]{0,1:T(8,128)}) %all-reduce.7.cloned.1.call-update) | async-done | bytes 65552 | tf_op jit(solution)/shard_map/psum | solution.py:16
  330.8 0.9 copy.15
  331.8 0.9 fusion.9
  332.6 11.7 %cholesky.44 = f32[128,128]{1,0:T(8,128)S(1)} custom-call(f32[128,128]{1,0:T(8,128)S(1)} %fusion.9), custom_call_target="Cholesky" | custom-call | tf_op jit(solution)/shard_map/jit(cholesky)/cholesky | solution.py:17
  344.4 0.6 compare_reduce_fusion.1
  345.0 0.7 fusion.2
  345.7 9.8 custom-call.8
  355.5 0.7 broadcast_multiply_fusion
  356.2 3.0 fusion.16
  359.2 0.0 all-reduce.9.cloned.1.call-update
  359.2 0.0 all-reduce.11.cloned.1.call-start
  359.2 107.4 %all-reduce.9.cloned.1.call-done = f32[128,512]{0,1:T(8,128)} async-done(((f32[128,512]{0,1:T(8,128)}), f32[128,512]{0,1:T(8,128)}) %all-reduce.9.cloned.1.call-update) | async-done | bytes 262160 | tf_op jit(solution)/shard_map/psum | solution.py:23
  466.6 0.0 all-reduce.11.cloned.1.call-update
  466.6 0.0 reduce-scatter.2.cloned.1.call-start
  466.7 98.3 %all-reduce.11.cloned.1.call-done = f32[128,512]{0,1:T(8,128)} async-done(((f32[128,512]{0,1:T(8,128)}), f32[128,512]{0,1:T(8,128)}) %all-reduce.11.cloned.1.call-update) | async-done | bytes 262160 | tf_op jit(solution)/shard_map/psum | solution.py:23
  565.0 6.8 fusion.10
  571.8 0.0 reduce-scatter.2.cloned.1.call-update
  571.8 0.0 copy-start.2
  571.8 0.3 all-reduce.13.cloned.1.call-start
  572.1 84.1 %reduce-scatter.2.cloned.1.call-done = f32[8,20,512]{2,0,1:T(8,128)} async-done(((f32[128,20,512]{2,0,1:T(8,128)}), f32[8,20,512]{2,0,1:T(8,128)}) %reduce-scatter.2.cloned.1.call-update) | async-done | bytes 327696 | tf_op jit(solution)/shard_map/reduce_scatter | solution.py:52
  656.2 1.2 copy.16
  657.4 0.0 copy-done.2
  657.4 0.4 fusion.17
  657.8 1.1 fusion.18
  658.9 0.0 all-reduce.13.cloned.1.call-update
  658.9 0.0 all-reduce.15.cloned.1.call-start
  659.0 243.5 %all-reduce.13.cloned.1.call-done = f32[128,128]{0,1:T(8,128)} async-done(((f32[128,128]{0,1:T(8,128)}), f32[128,128]{0,1:T(8,128)}) %all-reduce.13.cloned.1.call-update) | async-done | bytes 65552 | tf_op jit(solution)/shard_map/psum | solution.py:16
  902.5 0.9 copy.18
  903.4 0.9 fusion.6
  904.3 11.7 %cholesky.55 = f32[128,128]{1,0:T(8,128)S(1)} custom-call(f32[128,128]{1,0:T(8,128)S(1)} %fusion.6), custom_call_target="Cholesky" | custom-call | tf_op jit(solution)/shard_map/jit(cholesky)/cholesky | solution.py:17
  916.0 0.6 compare_reduce_fusion
  916.7 0.7 fusion.3
  917.3 9.8 custom-call.9
  927.1 0.2 broadcast_multiply_fusion.1
  927.4 1.1 fusion.19
  928.5 0.0 all-reduce.15.cloned.1.call-update
  928.5 0.0 all-reduce.17.cloned.1.call-start
  928.6 107.4 %all-reduce.15.cloned.1.call-done = f32[128,512]{1,0:T(8,128)} async-done(((f32[128,512]{1,0:T(8,128)}), f32[128,512]{1,0:T(8,128)}) %all-reduce.15.cloned.1.call-update) | async-done | bytes 262160 | tf_op jit(solution)/shard_map/psum | solution.py:23
  1036.0 0.0 all-reduce.17.cloned.1.call-update
  1036.0 0.8 copy.19
  1036.8 0.7 copy.20
  1037.5 96.9 %all-reduce.17.cloned.1.call-done = f32[128,512]{1,0:T(8,128)} async-done(((f32[128,512]{1,0:T(8,128)}), f32[128,512]{1,0:T(8,128)}) %all-reduce.17.cloned.1.call-update) | async-done | bytes 262160 | tf_op jit(solution)/shard_map/psum | solution.py:23
  1134.4 1.7 copy.31
  (5 shorter events, 0.1 us)
Async XLA Ops:
  7.2 1.3 copy-start
  7.2 3.4 copy-start.1
  7.2 323.6 %all-reduce.7.cloned.1.call-start = ((), (), s32[]{:S(2)}) async-start(), calls=%async_computation.1 | async-start | bytes 131072 | tf_op jit(solution)/shard_map/psum | solution.py:16
  94.1 372.6 %all-reduce.9.cloned.1.call-start = ((), (), s32[]{:S(2)}) async-start(), calls=%async_computation.2 | async-start | bytes 524288 | tf_op jit(solution)/shard_map/psum | solution.py:23
  359.2 205.8 %all-reduce.11.cloned.1.call-start = ((), (), s32[]{:S(2)}) async-start(), calls=%async_computation.3 | async-start | bytes 524288 | tf_op jit(solution)/shard_map/psum | solution.py:23
  466.6 189.5 %reduce-scatter.2.cloned.1.call-start = ((), (), s32[]{:S(2)}) async-start(), calls=%async_computation.4 | async-start | bytes 5570560 | tf_op jit(solution)/shard_map/reduce_scatter | solution.py:52
  571.8 85.6 %copy-start.2 = (f32[512,128]{1,0:T(8,128)S(1)}, f32[512,128]{1,0:T(8,128)}, u32[]{:S(2)}) copy-start(f32[512,128]{1,0:T(8,128)} %param.7) | copy-start | bytes 786436
  571.8 330.6 %all-reduce.13.cloned.1.call-start = ((), (), s32[]{:S(2)}) async-start(), calls=%async_computation.5 | async-start | bytes 131072 | tf_op jit(solution)/shard_map/psum | solution.py:16
  658.9 377.1 %all-reduce.15.cloned.1.call-start = ((), (), s32[]{:S(2)}) async-start(), calls=%async_computation.6 | async-start | bytes 524288 | tf_op jit(solution)/shard_map/psum | solution.py:23
  928.5 205.8 %all-reduce.17.cloned.1.call-start = ((), (), s32[]{:S(2)}) async-start(), calls=%async_computation.7 | async-start | bytes 524288 | tf_op jit(solution)/shard_map/psum | solution.py:23
Sparse Core Ops, SparseCore 0:
  94.2 236.5 all-reduce.6
  359.3 107.2 all-reduce.8
  469.8 95.1 all-reduce.10
  571.9 84.1 reduce-scatter.1
  662.1 240.3 all-reduce.12
  928.6 107.2 all-reduce.14
  1039.2 95.1 all-reduce.16
